TPU v7x, 256 devices: a whole 4x4x8 slice. The times are simulated.
256 devices in a mesh: tm: 64 (over y, x, z_lo, core), inp: 4 (over z_hi).
Axes of the slice: x: 4, y: 4, z: 8 (z_hi: 4, z_lo: 2; z = z_hi * 2 + z_lo), core: 2. Of those that a mesh axis runs over, the one named last changes fastest.
Arguments:
- voltages: bfloat16 [1024, 262144], P('inp', 'tm'), may hold values from -6 to 6
- input_gain: float32 [1024], P('inp'), may hold values from 0.5 to 2
- input_feed: int32 [1024], replicated, may hold values from 0 to 511
- beam_grid: int32 [1024], replicated, may hold values from 0 to 511
Outputs:
- visibilities: bfloat16 [512, 2, 1024, 1024], P(('tm', 'inp'))
- beam_power: float32 [512, 1024], P(('tm', 'inp'))
All inputs are finite; a program needn't handle non-finite values.
Results may differ from a plain program's by a relative error of at most 0.0034.
Values may be sent and summed in bfloat16 or wider, within the bound.
A program may use at most 64 MiB of HBM per device.

v0:
```python
import functools
import math

import jax
import jax.numpy as jnp
import numpy as np
from jax import lax
from jax.experimental import pallas as pl
from jax.experimental.pallas import tpu as pltpu
from jax.sharding import PartitionSpec as P

MESH = pl.DeviceIdType.MESH
L = 1024
CH = 512
TAPS = 4
GRID = 512
LANES = 128


def window_table():
    span = TAPS * L
    pos = np.arange(span).astype(np.float64)
    sinc_part = np.sinc((pos - span / 2) / L)
    hann_part = 0.5 - 0.5 * np.cos(2.0 * np.pi * pos / span)
    return (sinc_part * hann_part).reshape(TAPS, L).astype(np.float32)


def dft_table():
    step = np.arange(CH)[:, None] * np.arange(L)[None, :] % L
    radians = 2.0 * np.pi * step / L
    rows = np.stack([np.cos(radians), -np.sin(radians)], 1) / math.sqrt(L)
    return rows.reshape(2 * CH, L).astype(jnp.bfloat16)


def steer_tables(input_feed, beam_grid):
    phase = (input_feed[:, None] * beam_grid[None, :]) & (GRID - 1)
    turned = phase + GRID // 8
    quarter = (turned >> 7) & 3
    rest = (turned & 127) - GRID // 8
    x = rest.astype(jnp.float32) * (2.0 * math.pi / GRID)
    y = x * x
    sine = x * (1.0 + y * (-1.0 / 6 + y * (1.0 / 120 + y * (-1.0 / 5040 + y * (1.0 / 362880)))))
    cosine = 1.0 + y * (-0.5 + y * (1.0 / 24 + y * (-1.0 / 720 + y * (1.0 / 40320))))
    swap = (quarter & 1) == 1
    factor = 1.0 / math.sqrt(input_feed.shape[0])
    c_sign = jnp.where((quarter == 1) | (quarter == 2), -factor, factor)
    s_sign = jnp.where(quarter >= 2, factor, -factor)
    c = jnp.where(swap, sine, cosine) * c_sign
    s = jnp.where(swap, cosine, sine) * s_sign
    return c.astype(jnp.bfloat16), s.astype(jnp.bfloat16)


def exchange_kernel(n_time, n_inp, volt, halo, gain, window, table, recv, filt, wide, send, s_sem, r_sem, l_sem):
    total = n_time * n_inp
    rows = volt.shape[0]
    frames = volt.shape[1] // L
    chunks = rows // LANES
    tm = lax.axis_index("tm")
    inp = lax.axis_index("inp")
    me = tm * n_inp + inp

    barrier = pltpu.get_barrier_semaphore()

    def greet(s, carry):
        d = lax.rem(me + s, total)
        pl.semaphore_signal(barrier, inc=1, device_id={"tm": d // n_inp, "inp": lax.rem(d, n_inp)}, device_id_type=MESH)
        return carry

    lax.fori_loop(1, total, greet, 0)
    last = tm == n_time - 1
    step_rows = 16
    for c in range(chunks):
        for f in range(frames):

            def one(i, carry):
                at = pl.multiple_of(i * step_rows, step_rows)
                from_rows = pl.ds(c * LANES + at, step_rows)
                summed = None
                for tap in range(TAPS):
                    g = f + tap
                    if g < frames:
                        piece = volt[from_rows, g * L : (g + 1) * L].astype(jnp.float32)
                    else:
                        piece = halo[from_rows, (g - frames) * L : (g - frames + 1) * L].astype(jnp.float32)
                        piece = jnp.where(last, 0.0, piece)
                    term = piece * window[tap : tap + 1, :]
                    summed = term if summed is None else summed + term
                filt[pl.ds(f * LANES + at, step_rows), :] = (summed * gain[from_rows, :]).astype(jnp.bfloat16)
                return carry

            lax.fori_loop(0, LANES // step_rows, one, 0)
        block = 256
        for b in range(2 * CH // block):
            part = lax.dot_general(
                table[b * block : (b + 1) * block, :],
                filt[...],
                (((1,), (1,)), ((), ())),
                preferred_element_type=jnp.float32,
            )
            for f in range(frames):
                wide[pl.ds(f, block, stride=frames), :] = part[:, f * LANES : (f + 1) * LANES]
            n = block * frames // 16
            send[c * total + b * n : c * total + (b + 1) * n] = wide[...].astype(jnp.bfloat16).reshape(n, 16, LANES)
        if c == 0:
            pl.semaphore_wait(barrier, total - 1)
        slot = (inp * chunks + c) * n_time + tm

        def ship(s, carry):
            d = lax.rem(me + s, total)
            pltpu.make_async_remote_copy(
                send.at[c * total + d],
                recv.at[slot],
                s_sem,
                r_sem,
                device_id={"tm": d // n_inp, "inp": lax.rem(d, n_inp)},
                device_id_type=MESH,
            ).start()
            return carry

        lax.fori_loop(1, total, ship, 0)
        pltpu.make_async_copy(send.at[c * total + me], recv.at[slot], l_sem.at[c]).start()
    for c in range(chunks):
        slot = (inp * chunks + c) * n_time + tm
        pltpu.make_async_copy(send.at[c * total + me], recv.at[slot], l_sem.at[c]).wait()
    everything = pl.ds(0, chunks * (total - 1))
    pltpu.make_async_copy(send.at[everything], send.at[everything], s_sem).wait()
    pltpu.make_async_copy(recv.at[everything], recv.at[everything], r_sem).wait()


def exchange(volt, halo, gain, n_time, n_inp):
    rows = volt.shape[0]
    frames = volt.shape[1] // L
    chunks = rows // LANES
    blocks = chunks * n_time * n_inp
    vmem = pl.BlockSpec(memory_space=pltpu.VMEM)
    return pl.pallas_call(
        functools.partial(exchange_kernel, n_time, n_inp),
        name="exchange",
        out_shape=jax.ShapeDtypeStruct((blocks, 16, LANES), jnp.bfloat16),
        in_specs=[vmem] * 5,
        out_specs=vmem,
        scratch_shapes=[
            pltpu.VMEM((frames * LANES, L), jnp.bfloat16),
            pltpu.VMEM((256 * frames, LANES), jnp.float32),
            pltpu.VMEM((blocks, 16, LANES), jnp.bfloat16),
            pltpu.SemaphoreType.DMA,
            pltpu.SemaphoreType.DMA,
            pltpu.SemaphoreType.DMA((chunks,)),
        ],
        compiler_params=pltpu.CompilerParams(collective_id=0, has_side_effects=True, vmem_limit_bytes=40 << 20),
    )(volt, halo, gain, jnp.asarray(window_table()), jnp.asarray(dft_table()))


def products_kernel(groups, n_time, recv, cosine, sine, visible, power, spec, turn, spec_t, turn_t):
    j = pl.program_id(1)
    ch = pl.program_id(0)
    depth = n_time * 8

    @pl.when(j == 0)
    def _():
        sign = jnp.where(lax.broadcasted_iota(jnp.int32, (depth, LANES), 0) % 8 < 4, 1.0, -1.0)
        for g in range(groups):
            part = recv[g * n_time : (g + 1) * n_time, pl.ds(pl.multiple_of(ch * 8, 8), 8), :].reshape(depth, LANES)
            wide = part.astype(jnp.float32)
            swapped = pltpu.roll(wide.reshape(n_time, 8, LANES), 4, 1).reshape(depth, LANES) * sign
            lanes = slice(g * LANES, (g + 1) * LANES)
            spec[:, lanes] = part
            turn[:, lanes] = swapped.astype(jnp.bfloat16)
            spec_t[lanes, :] = wide.T.astype(jnp.bfloat16)
            turn_t[lanes, :] = swapped.T.astype(jnp.bfloat16)

    width = visible.shape[-1]
    cols = pl.ds(pl.multiple_of(j * width, width), width)
    right = spec[:, cols]
    scale = 2.0 / depth
    visible[0, 0] = (jnp.dot(spec_t[...], right, preferred_element_type=jnp.float32) * scale).astype(jnp.bfloat16)
    visible[0, 1] = (jnp.dot(turn_t[...], right, preferred_element_type=jnp.float32) * scale).astype(jnp.bfloat16)
    beams = jnp.dot(spec[...], cosine[:, cols], preferred_element_type=jnp.float32) + jnp.dot(
        turn[...], sine[:, cols], preferred_element_type=jnp.float32
    )
    power[0] = jnp.sum(beams * beams, axis=0, keepdims=True) * scale


def products(recv, cosine, sine, n_time):
    groups = recv.shape[0] // n_time
    inputs, beams = cosine.shape
    width = 256
    depth = n_time * 8
    vmem = pl.BlockSpec(memory_space=pltpu.VMEM)
    visible, power = pl.pallas_call(
        functools.partial(products_kernel, groups, n_time),
        name="products",
        grid=(2, inputs // width),
        out_shape=(
            jax.ShapeDtypeStruct((2, 2, inputs, inputs), jnp.bfloat16),
            jax.ShapeDtypeStruct((2, 1, beams), jnp.float32),
        ),
        in_specs=[vmem] * 3,
        out_specs=(
            pl.BlockSpec((1, 2, inputs, width), lambda c, j: (c, 0, 0, j)),
            pl.BlockSpec((1, 1, width), lambda c, j: (c, 0, j)),
        ),
        scratch_shapes=[
            pltpu.VMEM((depth, inputs), jnp.bfloat16),
            pltpu.VMEM((depth, inputs), jnp.bfloat16),
            pltpu.VMEM((inputs, depth), jnp.bfloat16),
            pltpu.VMEM((inputs, depth), jnp.bfloat16),
        ],
        compiler_params=pltpu.CompilerParams(vmem_limit_bytes=40 << 20),
    )(recv, cosine, sine)
    return visible, power.reshape(2, beams)


def on_device(voltages, input_gain, input_feed, beam_grid):
    n_time = lax.axis_size("tm")
    n_inp = lax.axis_size("inp")
    route = [(i + 1, i) for i in range(n_time - 1)]
    halo = lax.ppermute(voltages[:, : (TAPS - 1) * L], "tm", route)
    cosine, sine = steer_tables(input_feed, beam_grid)
    recv = exchange(voltages, halo, input_gain[:, None], n_time, n_inp)
    return products(recv, cosine, sine, n_time)


def solution(mesh):
    return jax.shard_map(
        on_device,
        mesh=mesh,
        in_specs=(P("inp", "tm"), P("inp"), P(), P()),
        out_specs=(P(("tm", "inp"), None, None, None), P(("tm", "inp"), None)),
        check_vma=False,
    )
```

profile of v0, /device:TPU:1, one launch (start us, length us, event | category | flops | bytes accessed | tf_op | source)
XLA Modules:
  0.0 105.3 jit_solution(12172169647889467926)
XLA Ops:
  0.6 0.0 copy-start.2
  0.6 0.0 copy-start
  0.7 2.8 %slice.3 = bf16[256,3072]{1,0:T(8,128)(2,1)} slice(bf16[256,4096]{1,0:T(8,128)(2,1)} %volt.1), slice={[0:256], [0:3072]} | slice | bytes 3145728 | tf_op jit(solution)/shard_map/slice | solution.py:218
  3.5 5.1 %collective-permute-start = (bf16[256,3072]{1,0:T(8,128)(2,1)}, bf16[256,3072]{1,0:T(8,128)(2,1)}, u32[]{:S(2)}, u32[]{:S(2)}) collective-permute-start(bf16[256,3072]{1,0:T(8,128)(2,1)} %slice.3), channel_id=1, source_target_pairs={{4,0},{8,4},{12,8},{16,12},{20,16},{24,20},{28,24},{32,28},{36,32}... | collective-permute-start | bytes 4718600 | tf_op jit(solution)/shard_map/ppermute | solution.py:218
  8.6 0.8 copy.8.gain
  9.4 0.0 copy-start.1
  9.4 6.6 %multiply_convert_fusion = (bf16[1024,1024]{1,0:T(8,128)(2,1)S(1)}, bf16[1024,1024]{1,0:T(8,128)(2,1)S(1)}) fusion(s32[1024]{0:T(1024)} %param.9, s32[1024]{0:T(1024)} %param.8), kind=kLoop, calls=%fused_computation | loop fusion | flops 42991616 | bytes 4202496 | tf_op jit(solution)/shard_map/convert_element_type | solution.py:50
  15.9 10.8 %collective-permute-done.halo = bf16[256,3072]{1,0:T(8,128)(2,1)} collective-permute-done((bf16[256,3072]{1,0:T(8,128)(2,1)}, bf16[256,3072]{1,0:T(8,128)(2,1)}, u32[]{:S(2)}, u32[]{:S(2)}) %collective-permute-start) | collective-permute-done | bytes 1572896 | tf_op jit(solution)/shard_map/ppermute | solution.py:218
  26.8 0.0 copy-done.2
  26.8 0.0 copy-done
  26.8 0.0 copy-done.1
  26.8 64.8 %exchange.1.recv = bf16[512,16,128]{2,1,0:T(8,128)(2,1)S(1)} custom-call(bf16[256,4096]{1,0:T(8,128)(2,1)S(1)} %copy-done, bf16[256,3072]{1,0:T(8,128)(2,1)} %collective-permute-done.halo, f32[256,1]{1,0:T(8,128)S(1)} %copy.8.gain, f32[4,1024]{1,0:T(4,128)S(1)} %copy-done.2, bf16[1024,1024]{1,0:T(8,128)(2,1)S(1)} %copy-done.1), custom_call_target="tpu_custom_call" | custom-call | tf_op jit(solution)/shard_map/exchange/pallas_call | solution.py:136
  91.6 13.1 %products.1 = (bf16[2,2,1024,1024]{3,2,1,0:T(8,128)(2,1)}, f32[2,1,1024]{2,1,0:T(1,128)S(1)}) custom-call(bf16[512,16,128]{2,1,0:T(8,128)(2,1)S(1)} %exchange.1.recv, bf16[1024,1024]{1,0:T(8,128)(2,1)S(1)} %get-tuple-element.7.cosine, bf16[1024,1024]{1,0:T(8,128)(2,1)S(1)} %get-tuple-element.6.sine), custom_call_target="tpu_custom_call" | custom-call | tf_op jit(solution)/shard_map/products/pallas_call | solution.py:190
  104.7 0.6 copy.11
Async XLA Ops:
  0.6 26.1 %copy-start.2 = (f32[4,1024]{1,0:T(4,128)S(1)}, f32[4,1024]{1,0:T(4,128)}, u32[]{:S(2)}) copy-start(f32[4,1024]{1,0:T(4,128)} %constant.44.clone.window) | copy-start | bytes 49156
  0.6 26.1 %copy-start = (bf16[256,4096]{1,0:T(8,128)(2,1)S(1)}, bf16[256,4096]{1,0:T(8,128)(2,1)}, u32[]{:S(2)}) copy-start(bf16[256,4096]{1,0:T(8,128)(2,1)} %volt.1) | copy-start | bytes 6291460
  3.5 23.3 %collective-permute-start = (bf16[256,3072]{1,0:T(8,128)(2,1)}, bf16[256,3072]{1,0:T(8,128)(2,1)}, u32[]{:S(2)}, u32[]{:S(2)}) collective-permute-start(bf16[256,3072]{1,0:T(8,128)(2,1)} %slice.3), channel_id=1, source_target_pairs={{4,0},{8,4},{12,8},{16,12},{20,16},{24,20},{28,24},{32,28},{36,32}... | collective-permute-start | bytes 4718600 | tf_op jit(solution)/shard_map/ppermute | solution.py:218
  9.4 17.4 %copy-start.1 = (bf16[1024,1024]{1,0:T(8,128)(2,1)S(1)}, bf16[1024,1024]{1,0:T(8,128)(2,1)}, u32[]{:S(2)}) copy-start(bf16[1024,1024]{1,0:T(8,128)(2,1)} %constant.45.clone.table) | copy-start | bytes 6291460
where the time goes:
time: 105 us
  Pallas kernels  77.9 us (74%)
  waiting for transfers between devices  10.8 us (10%)
  other arithmetic  6.55 us (6%)
  starting transfers between devices  5.1 us (5%)
  local copies, waits for them, and re-layouts  4.23 us (4%)
    pallas_call x1, Pallas kernels, exchange(): pl.pallas_call(functools.partial(exchange_kernel, n_time, n_inp), name='e...  64.8 us
    pallas_call x1, Pallas kernels, products(): pl.pallas_call(functools.partial(products_kernel, groups, n_time), name='...  13.1 us
    ppermute x1, waiting for transfers between devices, on_device(): halo = lax.ppermute(voltages[:, :(TAPS - 1) * L], 'tm', route)  10.8 us
    convert_element_type x1, other arithmetic, steer_tables(): return (c.astype(jnp.bfloat16), s.astype(jnp.bfloat16))  6.55 us
    ppermute x1, starting transfers between devices, on_device(): halo = lax.ppermute(voltages[:, :(TAPS - 1) * L], 'tm', route)  5.1 us
    slice x1, local copies, waits for them, and re-layouts, on_device(): halo = lax.ppermute(voltages[:, :(TAPS - 1) * L], 'tm', route)  2.8 us
  transfers between devices with their start and end apart: 1, of which 1 were waited for; matrix products, arithmetic and copies ran while one was open for 7% of the time, Pallas kernels for 0%

commit v1 on v0

v1 whole, which is shorter than its diff:
```python
import functools
import math

import jax
import jax.numpy as jnp
import numpy as np
from jax import lax
from jax.experimental import pallas as pl
from jax.experimental.pallas import tpu as pltpu
from jax.sharding import PartitionSpec as P

LOGICAL = pl.DeviceIdType.LOGICAL
L = 1024
CH = 512
TAPS = 4
GRID = 512
LANES = 128
PAIR = 2


def window_table():
    span = TAPS * L
    pos = np.arange(span).astype(np.float64)
    sinc_part = np.sinc((pos - span / 2) / L)
    hann_part = 0.5 - 0.5 * np.cos(2.0 * np.pi * pos / span)
    return (sinc_part * hann_part).reshape(TAPS, L).astype(np.float32)


def dft_table():
    step = np.arange(CH)[:, None] * np.arange(L)[None, :] % L
    radians = 2.0 * np.pi * step / L
    rows = np.stack([np.cos(radians), -np.sin(radians)], 1) / math.sqrt(L)
    return rows.reshape(2 * CH, L).astype(jnp.bfloat16)


def steer_block(phase, factor):
    phase = phase & (GRID - 1)
    turned = phase + GRID // 8
    quarter = (turned >> 7) & 3
    rest = (turned & 127) - GRID // 8
    x = rest.astype(jnp.float32) * (2.0 * math.pi / GRID)
    y = x * x
    sine = x * (1.0 + y * (-1.0 / 6 + y * (1.0 / 120 + y * (-1.0 / 5040 + y * (1.0 / 362880)))))
    cosine = 1.0 + y * (-0.5 + y * (1.0 / 24 + y * (-1.0 / 720 + y * (1.0 / 40320))))
    swap = (quarter & 1) == 1
    c_sign = jnp.where((quarter == 1) | (quarter == 2), -factor, factor)
    s_sign = jnp.where(quarter >= 2, factor, -factor)
    c = jnp.where(swap, sine, cosine) * c_sign
    s = jnp.where(swap, cosine, sine) * s_sign
    return c.astype(jnp.bfloat16), s.astype(jnp.bfloat16)


def arrange(recv, first, n_time, n_inp, spec, turn, spec_t, turn_t):
    width = recv.shape[2]
    half = n_time // 2
    rows = half * 8
    row = lax.broadcasted_iota(jnp.int32, (half, 8, width), 1)
    low = row < 4
    real = (row & 2) == 0
    for g in range(n_inp):
        lanes = slice(g * width, (g + 1) * width)
        got = recv[first + g * n_time : first + (g + 1) * n_time].astype(jnp.float32).reshape(half, 2, 8, width)
        even, odd = got[:, 0], got[:, 1]
        for ch in range(2):
            if ch == 0:
                y = jnp.where(low, even, pltpu.roll(odd, 4, 1))
            else:
                y = jnp.where(low, pltpu.roll(even, 4, 1), odd)
            z = jnp.where(real, pltpu.roll(y, 6, 1), -pltpu.roll(y, 2, 1))
            y = y.reshape(rows, width)
            z = z.reshape(rows, width)
            spec[ch, :, lanes] = y.astype(jnp.bfloat16)
            turn[ch, :, lanes] = z.astype(jnp.bfloat16)
            spec_t[ch, lanes, :] = y.T.astype(jnp.bfloat16)
            turn_t[ch, lanes, :] = z.T.astype(jnp.bfloat16)


def beam_sum(spec, turn, cosine, sine, ch, cols):
    beams = jnp.dot(spec[ch], cosine[:, cols], preferred_element_type=jnp.float32) + jnp.dot(
        turn[ch], sine[:, cols], preferred_element_type=jnp.float32
    )
    return jnp.sum(beams * beams, axis=0, keepdims=True)


def exchange_kernel(
    n_time,
    n_inp,
    volt,
    gain,
    window,
    table,
    feed,
    grid,
    recv,
    cosine,
    sine,
    sums,
    power,
    filt,
    wide,
    send,
    halo,
    gain_b,
    feed_b,
    spec,
    turn,
    spec_t,
    turn_t,
    s_sem,
    r_sem,
    hs_sem,
    hr_sem,
    l_sem,
):
    total = n_time * n_inp
    rows = volt.shape[0]
    inputs = feed.shape[1]
    frames = volt.shape[1] // L
    chunks = frames // PAIR
    tm = lax.axis_index("tm")
    inp = lax.axis_index("inp")
    me = tm * n_inp + inp
    barrier = pltpu.get_barrier_semaphore()

    def others(visit):
        def one(d, carry):
            visit(d)
            return carry

        lax.fori_loop(me + 1, total, one, 0)
        lax.fori_loop(0, me, one, 0)

    others(lambda d: pl.semaphore_signal(barrier, inc=1, device_id=d, device_id_type=LOGICAL))

    step_rows = 16

    def filter_frame(f):
        def one(i, carry):
            at = pl.ds(pl.multiple_of(i * step_rows, step_rows), step_rows)
            summed = None
            for tap in range(TAPS):
                g = f + tap
                if g < frames:
                    piece = volt[at, g * L : (g + 1) * L].astype(jnp.float32)
                else:
                    piece = halo[at, (g - frames) * L : (g - frames + 1) * L].astype(jnp.float32)
                term = piece * window[tap : tap + 1, :]
                summed = term if summed is None else summed + term
            scale = jnp.concatenate([gain_b[at, :]] * (L // LANES), 1)
            filt[at, :] = (summed * scale).astype(jnp.bfloat16)
            return carry

        lax.fori_loop(0, rows // step_rows, one, 0)

    def transform_frame(f):
        c, place = f // PAIR, f % PAIR
        block = 256
        for b in range(2 * CH // block):
            part = lax.dot_general(
                table[b * block : (b + 1) * block, :],
                filt[...],
                (((1,), (1,)), ((), ())),
                preferred_element_type=jnp.float32,
            )
            start = b * block * PAIR
            for h in range(rows // LANES):
                wide[h, pl.ds(start + place, block, stride=PAIR), :] = part[:, h * LANES : (h + 1) * LANES]
            if place == PAIR - 1:
                n = block * PAIR // 8
                for h in range(rows // LANES):
                    ready = wide[h, start : start + block * PAIR, :].astype(jnp.bfloat16).reshape(n, 8, LANES)
                    send[c * total + b * n : c * total + (b + 1) * n, :, h * LANES : (h + 1) * LANES] = ready

    def ship(c):
        slot = c * total + inp * n_time + tm

        def one(d):
            pltpu.make_async_remote_copy(
                send.at[c * total + d],
                recv.at[slot],
                s_sem.at[c],
                r_sem.at[c],
                device_id=d,
                device_id_type=LOGICAL,
            ).start()

        others(one)
        pltpu.make_async_copy(send.at[c * total + me], recv.at[slot], l_sem.at[c]).start()

    def arrived(c):
        slot = c * total + inp * n_time + tm
        pltpu.make_async_copy(send.at[c * total + me], recv.at[slot], l_sem.at[c]).wait()
        some = pl.ds(c * total, total - 1)
        pltpu.make_async_copy(recv.at[some], recv.at[some], r_sem.at[c]).wait()

    def left(c):
        some = pl.ds(c * total, total - 1)
        pltpu.make_async_copy(send.at[some], send.at[some], s_sem.at[c]).wait()

    def halo_copy(g):
        cols = pl.ds(g * L, L)
        back = lax.select(tm == 0, total - n_inp + inp, me - n_inp)
        return pltpu.make_async_remote_copy(
            volt.at[:, cols],
            halo.at[:, cols],
            hs_sem.at[g],
            hr_sem.at[g],
            device_id=back,
            device_id_type=LOGICAL,
        )

    def halo_ready(g):
        halo_copy(g).wait_recv()

        @pl.when(tm == n_time - 1)
        def _():
            halo[:, g * L : (g + 1) * L] = jnp.zeros((rows, L), jnp.bfloat16)

    gain_b[...] = jnp.broadcast_to(gain[...], (LANES, rows)).T
    feed_b[...] = jnp.broadcast_to(feed[...], (LANES, inputs)).T
    filter_frame(0)
    transform_frame(0)
    pl.semaphore_wait(barrier, total - 1)
    for g in range(TAPS - 1):
        halo_copy(g).start()

    def steer(i, carry):
        at = pl.ds(pl.multiple_of(i * step_rows, step_rows), step_rows)
        turns = jnp.concatenate([feed_b[at, :]] * (grid.shape[1] // LANES), 1) * grid[...]
        c, s = steer_block(turns, 1.0 / math.sqrt(inputs))
        cosine[at, :] = c
        sine[at, :] = s
        return carry

    lax.fori_loop(0, inputs // step_rows, steer, 0)
    for f in range(1, frames):
        halo_ready(f - 1)
        filter_frame(f)
        transform_frame(f)
        if f % PAIR == PAIR - 1:
            ship(f // PAIR)

    for c in range(chunks - 1):
        arrived(c)
        arrange(recv, c * total, n_time, n_inp, spec, turn, spec_t, turn_t)
        width = 256

        def products(j, carry):
            cols = pl.ds(pl.multiple_of(j * width, width), width)
            for ch in range(2):
                right = spec[ch, :, cols]
                sums[ch, 0, :, cols] = jnp.dot(spec_t[ch], right, preferred_element_type=jnp.float32)
                sums[ch, 1, :, cols] = jnp.dot(turn_t[ch], right, preferred_element_type=jnp.float32)
                power[ch, :, cols] = beam_sum(spec, turn, cosine, sine, ch, cols)
            return carry

        lax.fori_loop(0, inputs // width, products, 0)
    arrived(chunks - 1)
    for c in range(chunks):
        left(c)
    for g in range(TAPS - 1):
        halo_copy(g).wait_send()


def exchange(volt, gain, feed, grid, n_time, n_inp):
    rows = volt.shape[0]
    frames = volt.shape[1] // L
    chunks = frames // PAIR
    blocks = chunks * n_time * n_inp
    inputs = feed.shape[1]
    beams = grid.shape[1]
    depth = n_time * 4
    vmem = pl.BlockSpec(memory_space=pltpu.VMEM)
    dma = pltpu.SemaphoreType.DMA
    return pl.pallas_call(
        functools.partial(exchange_kernel, n_time, n_inp),
        name="exchange",
        out_shape=(
            jax.ShapeDtypeStruct((blocks, 8, rows), jnp.bfloat16),
            jax.ShapeDtypeStruct((inputs, beams), jnp.bfloat16),
            jax.ShapeDtypeStruct((inputs, beams), jnp.bfloat16),
            jax.ShapeDtypeStruct((2, 2, inputs, inputs), jnp.float32),
            jax.ShapeDtypeStruct((2, 1, beams), jnp.float32),
        ),
        in_specs=[vmem] * 6,
        out_specs=(vmem,) * 5,
        scratch_shapes=[
            pltpu.VMEM((rows, L), jnp.bfloat16),
            pltpu.VMEM((rows // LANES, 2 * CH * PAIR, LANES), jnp.float32),
            pltpu.VMEM((blocks, 8, rows), jnp.bfloat16),
            pltpu.VMEM((rows, (TAPS - 1) * L), jnp.bfloat16),
            pltpu.VMEM((rows, LANES), jnp.float32),
            pltpu.VMEM((inputs, LANES), jnp.int32),
            pltpu.VMEM((2, depth, inputs), jnp.bfloat16),
            pltpu.VMEM((2, depth, inputs), jnp.bfloat16),
            pltpu.VMEM((2, inputs, depth), jnp.bfloat16),
            pltpu.VMEM((2, inputs, depth), jnp.bfloat16),
            dma((chunks,)),
            dma((chunks,)),
            dma((TAPS - 1,)),
            dma((TAPS - 1,)),
            dma((chunks,)),
        ],
        compiler_params=pltpu.CompilerParams(collective_id=0, has_side_effects=True, vmem_limit_bytes=24 << 20),
    )(volt, gain, jnp.asarray(window_table()), jnp.asarray(dft_table()), feed, grid)


def products_kernel(n_time, n_inp, recv, cosine, sine, sums, part, visible, power, spec, turn, spec_t, turn_t):
    ch = pl.program_id(0)
    j = pl.program_id(1)

    @pl.when((ch == 0) & (j == 0))
    def _():
        arrange(recv, n_time * n_inp, n_time, n_inp, spec, turn, spec_t, turn_t)

    width = visible.shape[-1]
    cols = pl.ds(pl.multiple_of(j * width, width), width)
    right = spec[ch, :, cols]
    scale = 1.0 / (4 * n_time)
    for p, left in ((0, spec_t), (1, turn_t)):
        total = sums[ch, p, :, cols] + jnp.dot(left[ch], right, preferred_element_type=jnp.float32)
        visible[0, p] = (total * scale).astype(jnp.bfloat16)
    power[pl.ds(ch, 1), cols] = (part[ch, :, cols] + beam_sum(spec, turn, cosine, sine, ch, cols)) * scale


def products(recv, cosine, sine, sums, part, n_time, n_inp):
    inputs, beams = cosine.shape
    width = 256
    depth = n_time * 4
    vmem = pl.BlockSpec(memory_space=pltpu.VMEM)
    return pl.pallas_call(
        functools.partial(products_kernel, n_time, n_inp),
        name="products",
        grid=(2, inputs // width),
        out_shape=(
            jax.ShapeDtypeStruct((2, 2, inputs, inputs), jnp.bfloat16),
            jax.ShapeDtypeStruct((2, beams), jnp.float32),
        ),
        in_specs=[vmem] * 5,
        out_specs=(
            pl.BlockSpec((1, 2, inputs, width), lambda c, j: (c, 0, 0, j)),
            vmem,
        ),
        scratch_shapes=[
            pltpu.VMEM((2, depth, inputs), jnp.bfloat16),
            pltpu.VMEM((2, depth, inputs), jnp.bfloat16),
            pltpu.VMEM((2, inputs, depth), jnp.bfloat16),
            pltpu.VMEM((2, inputs, depth), jnp.bfloat16),
        ],
        compiler_params=pltpu.CompilerParams(vmem_limit_bytes=12 << 20),
    )(recv, cosine, sine, sums, part)


def on_device(voltages, input_gain, input_feed, beam_grid):
    n_time = lax.axis_size("tm")
    n_inp = lax.axis_size("inp")
    got = exchange(voltages, input_gain[None], input_feed[None], beam_grid[None], n_time, n_inp)
    return products(*got, n_time, n_inp)


def solution(mesh):
    return jax.shard_map(
        on_device,
        mesh=mesh,
        in_specs=(P("inp", "tm"), P("inp"), P(), P()),
        out_specs=(P(("tm", "inp"), None, None, None), P(("tm", "inp"), None)),
        check_vma=False,
    )
```

time: 105 us -> 95 us (0.905)
  waiting for transfers between devices: 10.8 us -> 0 us
  Pallas kernels: 77.9 us -> 88.1 us
  other arithmetic: 6.55 us -> 0 us
  starting transfers between devices: 5.1 us -> 0 us
  local copies, waits for them, and re-layouts: 4.23 us -> 5.94 us
    pallas_call x1, Pallas kernels: 64.8 us -> 79.5 us  [exchange(): pl.pallas_call(functools.partial(exchange_kernel, n_time, n_inp), name='e...]
    ppermute x1 -> x0, waiting for transfers between devices: 10.8 us -> none  [on_device(): halo = lax.ppermute(voltages[:, :(TAPS - 1) * L], 'tm', route)]
    convert_element_type x1 -> x0, other arithmetic: 6.55 us -> none  [steer_tables(): return (c.astype(jnp.bfloat16), s.astype(jnp.bfloat16))]
    unnamed x7 -> x12, local copies, waits for them, and re-layouts: 0.62 us -> 5.94 us
    ppermute x1 -> x0, starting transfers between devices: 5.1 us -> none  [on_device(): halo = lax.ppermute(voltages[:, :(TAPS - 1) * L], 'tm', route)]
    pallas_call x1, Pallas kernels: 13.1 us -> 8.6 us  [products(): pl.pallas_call(functools.partial(products_kernel, n_time, n_inp), name='p...]
    slice x1 -> x0, local copies, waits for them, and re-layouts: 2.8 us -> none  [on_device(): halo = lax.ppermute(voltages[:, :(TAPS - 1) * L], 'tm', route)]
  transfers between devices with their start and end apart: 1 -> 0, of which waited for: 1 -> 0; matrix products, arithmetic and copies ran while one was open for 7% -> 0% of each run, Pallas kernels for 0% -> 0%
where the time goes in v1:
time: 95 us; the launch traced here: 94.7 us
  Pallas kernels  88.1 us (93%)
  local copies, waits for them, and re-layouts  5.94 us (6%)
    pallas_call x1, Pallas kernels, exchange(): pl.pallas_call(functools.partial(exchange_kernel, n_time, n_inp), name='e...  79.5 us
    pallas_call x1, Pallas kernels, products(): pl.pallas_call(functools.partial(products_kernel, n_time, n_inp), name='p...  8.6 us
    unnamed x12, local copies, waits for them, and re-layouts  5.94 us

profile of v1, /device:TPU:1, one launch (start us, length us, event | category | flops | bytes accessed | tf_op | source)
XLA Modules:
  0.0 94.7 jit_solution(16573653707401067758)
XLA Ops:
  0.6 0.0 copy-start
  0.6 1.6 %copy-done = bf16[256,4096]{1,0:T(8,128)(2,1)S(1)} copy-done((bf16[256,4096]{1,0:T(8,128)(2,1)S(1)}, bf16[256,4096]{1,0:T(8,128)(2,1)}, u32[]{:S(2)}) %copy-start) | copy-done | bytes 2097176
  2.2 0.0 copy-start.1
  2.2 1.6 %copy-done.1 = bf16[1024,1024]{1,0:T(8,128)(2,1)S(1)} copy-done((bf16[1024,1024]{1,0:T(8,128)(2,1)S(1)}, bf16[1024,1024]{1,0:T(8,128)(2,1)}, u32[]{:S(2)}) %copy-start.1) | copy-done | bytes 2097176
  3.8 0.0 copy-start.2
  3.8 0.7 copy-done.2
  4.5 0.0 copy-start.3
  4.5 0.7 copy-done.3
  5.2 0.0 copy-start.4
  5.2 0.7 copy-done.4
  5.9 0.0 copy-start.5
  5.9 0.7 copy-done.5
  6.6 79.5 %exchange.1 = (bf16[512,8,256]{2,1,0:T(8,128)(2,1)S(1)}, bf16[1024,1024]{1,0:T(8,128)(2,1)S(1)}, bf16[1024,1024]{1,0:T(8,128)(2,1)S(1)}, f32[2,2,1024,1024]{3,2,1,0:T(8,128)S(1)}, f32[2,1,1024]{2,1,0:T(1,128)S(1)}) custom-call(bf16[256,4096]{1,0:T(8,128)(2,1)S(1)} %copy-done, f32[1,256]{1,0:T(1,128)S(1)} %bitcast.5, f32[4,1024]{1,0:T(4,128)S(1)} %copy-done.2, ...), custom_call_target="tpu_custom_call" | custom-call | tf_op jit(solution)/shard_map/exchange/pallas_call | solution.py:275
  86.1 8.6 %products.1 = (bf16[2,2,1024,1024]{3,2,1,0:T(8,128)(2,1)}, f32[2,1024]{1,0:T(2,128)}) custom-call(bf16[512,8,256]{2,1,0:T(8,128)(2,1)S(1)} %get-tuple-element.7.recv, bf16[1024,1024]{1,0:T(8,128)(2,1)S(1)} %get-tuple-element.8.cosine, bf16[1024,1024]{1,0:T(8,128)(2,1)S(1)} %get-tuple-element.9.sine, f32[2,2,1024,1024]{3,2,1,0:T(8,128)S(1)} %get-tuple-element.10.sums, ...), custom_call_target="tpu_custom_call" | custom-call | tf_op jit(solution)/shard_map/products/pallas_call | solution.py:331
Async XLA Ops:
  0.6 1.6 %copy-start = (bf16[256,4096]{1,0:T(8,128)(2,1)S(1)}, bf16[256,4096]{1,0:T(8,128)(2,1)}, u32[]{:S(2)}) copy-start(bf16[256,4096]{1,0:T(8,128)(2,1)} %volt.1) | copy-start | bytes 6291460
  2.2 1.6 %copy-start.1 = (bf16[1024,1024]{1,0:T(8,128)(2,1)S(1)}, bf16[1024,1024]{1,0:T(8,128)(2,1)}, u32[]{:S(2)}) copy-start(bf16[1024,1024]{1,0:T(8,128)(2,1)} %constant.5.clone.table) | copy-start | bytes 6291460
  3.8 0.7 copy-start.2
  4.5 0.7 copy-start.3
  5.2 0.7 copy-start.4
  5.9 0.7 copy-start.5

commit v2 on v1

--- a/solution.py
+++ b/solution.py
@@ -85,17 +85,23 @@
 def exchange_kernel(
     n_time,
     n_inp,
+    volt_h,
+    gain_h,
+    window_h,
+    table_h,
+    feed_h,
+    grid_h,
+    recv,
+    cosine,
+    sine,
+    sums,
+    power,
     volt,
     gain,
     window,
     table,
     feed,
     grid,
-    recv,
-    cosine,
-    sine,
-    sums,
-    power,
     filt,
     wide,
     send,
@@ -111,6 +117,7 @@
     hs_sem,
     hr_sem,
     l_sem,
+    in_sem,
 ):
     total = n_time * n_inp
     rows = volt.shape[0]
@@ -121,6 +128,14 @@
     inp = lax.axis_index("inp")
     me = tm * n_inp + inp
     barrier = pltpu.get_barrier_semaphore()
+    loads = [
+        pltpu.make_async_copy(there, here, in_sem.at[i])
+        for i, (there, here) in enumerate(
+            ((volt_h, volt), (window_h, window), (gain_h, gain), (feed_h, feed), (grid_h, grid), (table_h, table))
+        )
+    ]
+    for load in loads:
+        load.start()
 
     def others(visit):
         def one(d, carry):
@@ -130,7 +145,8 @@
         lax.fori_loop(me + 1, total, one, 0)
         lax.fori_loop(0, me, one, 0)
 
-    others(lambda d: pl.semaphore_signal(barrier, inc=1, device_id=d, device_id_type=LOGICAL))
+    with jax.named_scope("greet"):
+        others(lambda d: pl.semaphore_signal(barrier, inc=1, device_id=d, device_id_type=LOGICAL))
 
     step_rows = 16
 
@@ -216,11 +232,17 @@
         def _():
             halo[:, g * L : (g + 1) * L] = jnp.zeros((rows, L), jnp.bfloat16)
 
-    gain_b[...] = jnp.broadcast_to(gain[...], (LANES, rows)).T
-    feed_b[...] = jnp.broadcast_to(feed[...], (LANES, inputs)).T
-    filter_frame(0)
-    transform_frame(0)
-    pl.semaphore_wait(barrier, total - 1)
+    with jax.named_scope("load"):
+        for load in loads:
+            load.wait()
+        gain_b[...] = jnp.broadcast_to(gain[...], (LANES, rows)).T
+        feed_b[...] = jnp.broadcast_to(feed[...], (LANES, inputs)).T
+    with jax.named_scope("filter0"):
+        filter_frame(0)
+    with jax.named_scope("transform0"):
+        transform_frame(0)
+    with jax.named_scope("barrier"):
+        pl.semaphore_wait(barrier, total - 1)
     for g in range(TAPS - 1):
         halo_copy(g).start()
 
@@ -232,17 +254,24 @@
         sine[at, :] = s
         return carry
 
-    lax.fori_loop(0, inputs // step_rows, steer, 0)
+    with jax.named_scope("steer"):
+        lax.fori_loop(0, inputs // step_rows, steer, 0)
     for f in range(1, frames):
-        halo_ready(f - 1)
-        filter_frame(f)
-        transform_frame(f)
+        with jax.named_scope(f"halo{f}"):
+            halo_ready(f - 1)
+        with jax.named_scope(f"filter{f}"):
+            filter_frame(f)
+        with jax.named_scope(f"transform{f}"):
+            transform_frame(f)
         if f % PAIR == PAIR - 1:
-            ship(f // PAIR)
+            with jax.named_scope(f"ship{f}"):
+                ship(f // PAIR)
 
     for c in range(chunks - 1):
-        arrived(c)
-        arrange(recv, c * total, n_time, n_inp, spec, turn, spec_t, turn_t)
+        with jax.named_scope("arrive"):
+            arrived(c)
+        with jax.named_scope("arrange"):
+            arrange(recv, c * total, n_time, n_inp, spec, turn, spec_t, turn_t)
         width = 256
 
         def products(j, carry):
@@ -254,12 +283,15 @@
                 power[ch, :, cols] = beam_sum(spec, turn, cosine, sine, ch, cols)
             return carry
 
-        lax.fori_loop(0, inputs // width, products, 0)
-    arrived(chunks - 1)
-    for c in range(chunks):
-        left(c)
-    for g in range(TAPS - 1):
-        halo_copy(g).wait_send()
+        with jax.named_scope("products"):
+            lax.fori_loop(0, inputs // width, products, 0)
+    with jax.named_scope("final"):
+        arrived(chunks - 1)
+    with jax.named_scope("left"):
+        for c in range(chunks):
+            left(c)
+        for g in range(TAPS - 1):
+            halo_copy(g).wait_send()
 
 
 def exchange(volt, gain, feed, grid, n_time, n_inp):
@@ -282,9 +314,15 @@
             jax.ShapeDtypeStruct((2, 2, inputs, inputs), jnp.float32),
             jax.ShapeDtypeStruct((2, 1, beams), jnp.float32),
         ),
-        in_specs=[vmem] * 6,
+        in_specs=[pl.BlockSpec(memory_space=pltpu.HBM)] * 6,
         out_specs=(vmem,) * 5,
         scratch_shapes=[
+            pltpu.VMEM(volt.shape, volt.dtype),
+            pltpu.VMEM(gain.shape, gain.dtype),
+            pltpu.VMEM((TAPS, L), jnp.float32),
+            pltpu.VMEM((2 * CH, L), jnp.bfloat16),
+            pltpu.VMEM(feed.shape, feed.dtype),
+            pltpu.VMEM(grid.shape, grid.dtype),
             pltpu.VMEM((rows, L), jnp.bfloat16),
             pltpu.VMEM((rows // LANES, 2 * CH * PAIR, LANES), jnp.float32),
             pltpu.VMEM((blocks, 8, rows), jnp.bfloat16),
@@ -300,9 +338,10 @@
             dma((TAPS - 1,)),
             dma((TAPS - 1,)),
             dma((chunks,)),
+            dma((6,)),
         ],
         compiler_params=pltpu.CompilerParams(collective_id=0, has_side_effects=True, vmem_limit_bytes=24 << 20),
-    )(volt, gain, jnp.asarray(window_table()), jnp.asarray(dft_table()), feed, grid)
+    )(*(pltpu.with_memory_space_constraint(a, pltpu.HBM) for a in (volt, gain, jnp.asarray(window_table()), jnp.asarray(dft_table()), feed, grid)))
 
 
 def products_kernel(n_time, n_inp, recv, cosine, sine, sums, part, visible, power, spec, turn, spec_t, turn_t):

time: 95 us -> 89.2 us (0.939)
  local copies, waits for them, and re-layouts: 5.94 us -> 0 us
    unnamed x12 -> x0, local copies, waits for them, and re-layouts: 5.94 us -> none
where the time goes in v2:
time: 89.2 us; the launch traced here: 89.1 us
  Pallas kernels  88.4 us (99%)
    pallas_call x1, Pallas kernels, exchange(): pl.pallas_call(functools.partial(exchange_kernel, n_time, n_inp), name='e...  79.9 us
    pallas_call x1, Pallas kernels, products(): pl.pallas_call(functools.partial(products_kernel, n_time, n_inp), name='p...  8.58 us

profile of v2, /device:TPU:1, one launch (start us, length us, event | category | flops | bytes accessed | tf_op | source)
XLA Modules:
  0.0 89.1 jit_solution(12222099253166461918)
XLA Ops:
  0.6 79.9 %exchange.1 = (bf16[512,8,256]{2,1,0:T(8,128)(2,1)S(1)}, bf16[1024,1024]{1,0:T(8,128)(2,1)S(1)}, bf16[1024,1024]{1,0:T(8,128)(2,1)S(1)}, f32[2,2,1024,1024]{3,2,1,0:T(8,128)S(1)}, f32[2,1,1024]{2,1,0:T(1,128)S(1)}) custom-call(bf16[256,4096]{1,0:T(8,128)(2,1)} %volt_h.1, f32[1,256]{1,0:T(1,128)} %bitcast.5, f32[4,1024]{1,0:T(4,128)} %constant.4.clone.window_h, ...), custom_call_target="tpu_custom_call" | custom-call | tf_op jit(solution)/shard_map/exchange/pallas_call | solution.py:307
  80.5 8.6 %products.1 = (bf16[2,2,1024,1024]{3,2,1,0:T(8,128)(2,1)}, f32[2,1024]{1,0:T(2,128)}) custom-call(bf16[512,8,256]{2,1,0:T(8,128)(2,1)S(1)} %get-tuple-element.7.recv, bf16[1024,1024]{1,0:T(8,128)(2,1)S(1)} %get-tuple-element.8.cosine, bf16[1024,1024]{1,0:T(8,128)(2,1)S(1)} %get-tuple-element.9.sine, f32[2,2,1024,1024]{3,2,1,0:T(8,128)S(1)} %get-tuple-element.10.sums, ...), custom_call_target="tpu_custom_call" | custom-call | tf_op jit(solution)/shard_map/products/pallas_call | solution.py:370

commit v3 on v2

--- a/solution.py
+++ b/solution.py
@@ -26,10 +26,11 @@
     return (sinc_part * hann_part).reshape(TAPS, L).astype(np.float32)
 
 
-def dft_table():
+def dft_table(n_time, n_inp):
     step = np.arange(CH)[:, None] * np.arange(L)[None, :] % L
     radians = 2.0 * np.pi * step / L
     rows = np.stack([np.cos(radians), -np.sin(radians)], 1) / math.sqrt(L)
+    rows = rows.reshape(n_time // 4, 2, 2, n_inp, -1, L).transpose(3, 1, 0, 2, 4, 5)
     return rows.reshape(2 * CH, L).astype(jnp.bfloat16)
 
 
@@ -105,7 +106,11 @@
     filt,
     wide,
     send,
+    send_b,
     halo,
+    split,
+    outward,
+    inward,
     gain_b,
     feed_b,
     spec,
@@ -113,10 +118,12 @@
     spec_t,
     turn_t,
     s_sem,
+    b_sem,
     r_sem,
     hs_sem,
     hr_sem,
-    l_sem,
+    xs_sem,
+    xr_sem,
     in_sem,
 ):
     total = n_time * n_inp
@@ -124,9 +131,22 @@
     inputs = feed.shape[1]
     frames = volt.shape[1] // L
     chunks = frames // PAIR
+    n_yx, n_z = n_time // 4, 2 * n_inp
+    sides = n_z // 2
+    group = 2 * CH // n_z
+    owners = group // 4
     tm = lax.axis_index("tm")
     inp = lax.axis_index("inp")
     me = tm * n_inp + inp
+    core = lax.rem(tm, 2)
+    z_lo = lax.rem(tm // 2, 2)
+    yx = tm // 4
+    z = 2 * inp + z_lo
+    way = 2 * z_lo - 1
+    kept = [lax.rem(z + way * t + n_z, n_z) for t in range(sides)]
+    given = [lax.rem(z - way * (t + 1) + n_z, n_z) for t in range(sides)]
+    partner_tm = lax.rem(tm + 2 * core - 1 + n_time, n_time)
+    source_tm = lax.rem(tm + core - 1 + n_time, n_time)
     barrier = pltpu.get_barrier_semaphore()
     loads = [
         pltpu.make_async_copy(there, here, in_sem.at[i])
@@ -137,114 +157,173 @@
     for load in loads:
         load.start()
 
-    def others(visit):
-        def one(d, carry):
-            visit(d)
-            return carry
-
-        lax.fori_loop(me + 1, total, one, 0)
-        lax.fori_loop(0, me, one, 0)
+    def greet(d, carry):
+        pl.semaphore_signal(barrier, inc=1, device_id=d, device_id_type=LOGICAL)
+        return carry
 
     with jax.named_scope("greet"):
-        others(lambda d: pl.semaphore_signal(barrier, inc=1, device_id=d, device_id_type=LOGICAL))
+        lax.fori_loop(me + 1, total, greet, 0)
+        lax.fori_loop(0, me, greet, 0)
 
     step_rows = 16
 
-    def filter_frame(f):
+    def filter_frame(f, kind):
         def one(i, carry):
             at = pl.ds(pl.multiple_of(i * step_rows, step_rows), step_rows)
             summed = None
             for tap in range(TAPS):
                 g = f + tap
-                if g < frames:
-                    piece = volt[at, g * L : (g + 1) * L].astype(jnp.float32)
+                if (kind == "near" and g >= frames) or (kind == "far" and g < frames):
+                    continue
+                if kind == "full" and g >= frames:
+                    piece = halo[at, (g - frames) * L : (g - frames + 1) * L]
                 else:
-                    piece = halo[at, (g - frames) * L : (g - frames + 1) * L].astype(jnp.float32)
-                term = piece * window[tap : tap + 1, :]
+                    piece = volt[at, g % frames * L : (g % frames + 1) * L]
+                term = piece.astype(jnp.float32) * window[tap : tap + 1, :]
                 summed = term if summed is None else summed + term
-            scale = jnp.concatenate([gain_b[at, :]] * (L // LANES), 1)
+            scale = gain_b[at, :]
+            if kind == "far":
+                scale = jnp.where(tm == 0, 0.0, scale)
+            scale = jnp.concatenate([scale] * (L // LANES), 1)
             filt[at, :] = (summed * scale).astype(jnp.bfloat16)
             return carry
 
         lax.fori_loop(0, rows // step_rows, one, 0)
 
-    def transform_frame(f):
-        c, place = f // PAIR, f % PAIR
-        block = 256
+    block = 256
+
+    def spectrum(b):
+        return lax.dot_general(
+            table[pl.ds(b * block, block), :], filt[...], (((1,), (1,)), ((), ())), preferred_element_type=jnp.float32
+        )
+
+    def pack(part, place, first, count, target, at):
+        for h in range(rows // LANES):
+            wide[h, pl.ds(first * PAIR + place, count, stride=PAIR), :] = part[:, h * LANES : (h + 1) * LANES]
+        if place == PAIR - 1:
+            n = count * PAIR // 8
+            for h in range(rows // LANES):
+                ready = wide[h, first * PAIR : (first + count) * PAIR, :].astype(jnp.bfloat16).reshape(n, 8, LANES)
+                target[at : at + n, :, h * LANES : (h + 1) * LANES] = ready
+
+    def transform_whole(f):
         for b in range(2 * CH // block):
-            part = lax.dot_general(
-                table[b * block : (b + 1) * block, :],
-                filt[...],
-                (((1,), (1,)), ((), ())),
-                preferred_element_type=jnp.float32,
-            )
-            start = b * block * PAIR
-            for h in range(rows // LANES):
-                wide[h, pl.ds(start + place, block, stride=PAIR), :] = part[:, h * LANES : (h + 1) * LANES]
-            if place == PAIR - 1:
-                n = block * PAIR // 8
-                for h in range(rows // LANES):
-                    ready = wide[h, start : start + block * PAIR, :].astype(jnp.bfloat16).reshape(n, 8, LANES)
-                    send[c * total + b * n : c * total + (b + 1) * n, :, h * LANES : (h + 1) * LANES] = ready
-
-    def ship(c):
-        slot = c * total + inp * n_time + tm
-
-        def one(d):
+            pack(spectrum(b), f % PAIR, b * block, block, send, f // PAIR * total + b * block // 4)
+
+    def transform_part(f):
+        for b in range(2 * CH // block):
+            split[f, b * block : (b + 1) * block, :] = spectrum(b)
+        for t in range(sides):
+            at = pl.ds(pl.multiple_of(given[t] * group, group), group)
+            outward[f, t] = split[f, at, :].astype(jnp.bfloat16)
+
+    def combine(f):
+        for t in range(sides):
+            at = pl.ds(pl.multiple_of(kept[t] * group, group), group)
+            part = split[f, at, :] + inward[f, t].astype(jnp.float32)
+            pack(part, f % PAIR, t * group, group, send_b, f // PAIR * sides * owners + t * owners)
+
+    def ship(source, starts, levels, source_tm, c, sem):
+        slot = c * total + inp * n_time + source_tm
+        firsts = [lax.rem(v, 2) * 2 * n_inp + v // 2 for v in levels]
+
+        def copy(row, i, side):
             pltpu.make_async_remote_copy(
-                send.at[c * total + d],
+                source.at[starts[i] + row * 2 + side],
                 recv.at[slot],
-                s_sem.at[c],
+                sem.at[c],
                 r_sem.at[c],
-                device_id=d,
+                device_id=row * 4 * n_inp + firsts[i] + side * n_inp,
                 device_id_type=LOGICAL,
             ).start()
 
-        others(one)
-        pltpu.make_async_copy(send.at[c * total + me], recv.at[slot], l_sem.at[c]).start()
+        def one(row, carry):
+            for i in range(len(levels)):
+                for side in range(2):
+                    copy(row, i, side)
+            return carry
+
+        lax.fori_loop(yx + 1, n_yx, one, 0)
+        copy(yx, 0, 1 - core)
+        for i in range(1, len(levels)):
+            for side in range(2):
+                copy(yx, i, side)
+        lax.fori_loop(0, yx, one, 0)
+        pltpu.make_async_copy(source.at[starts[0] + yx * 2 + core], recv.at[slot], r_sem.at[c]).start()
 
     def arrived(c):
-        slot = c * total + inp * n_time + tm
-        pltpu.make_async_copy(send.at[c * total + me], recv.at[slot], l_sem.at[c]).wait()
-        some = pl.ds(c * total, total - 1)
+        some = pl.ds(c * total, total)
         pltpu.make_async_copy(recv.at[some], recv.at[some], r_sem.at[c]).wait()
-
-    def left(c):
-        some = pl.ds(c * total, total - 1)
-        pltpu.make_async_copy(send.at[some], send.at[some], s_sem.at[c]).wait()
 
     def halo_copy(g):
         cols = pl.ds(g * L, L)
-        back = lax.select(tm == 0, total - n_inp + inp, me - n_inp)
         return pltpu.make_async_remote_copy(
             volt.at[:, cols],
             halo.at[:, cols],
             hs_sem.at[g],
             hr_sem.at[g],
-            device_id=back,
+            device_id=me - n_inp,
             device_id_type=LOGICAL,
         )
 
-    def halo_ready(g):
-        halo_copy(g).wait_recv()
-
-        @pl.when(tm == n_time - 1)
-        def _():
-            halo[:, g * L : (g + 1) * L] = jnp.zeros((rows, L), jnp.bfloat16)
+    def part_copy(f):
+        return pltpu.make_async_remote_copy(
+            outward.at[f],
+            inward.at[f],
+            xs_sem.at[f],
+            xr_sem.at[f],
+            device_id=partner_tm * n_inp + inp,
+            device_id_type=LOGICAL,
+        )
 
     with jax.named_scope("load"):
         for load in loads:
             load.wait()
         gain_b[...] = jnp.broadcast_to(gain[...], (LANES, rows)).T
         feed_b[...] = jnp.broadcast_to(feed[...], (LANES, inputs)).T
-    with jax.named_scope("filter0"):
-        filter_frame(0)
-    with jax.named_scope("transform0"):
-        transform_frame(0)
+
+    @pl.when(core == 1)
+    def _():
+        with jax.named_scope("near"):
+            inward[0] = jnp.zeros(inward.shape[1:], inward.dtype)
+            for f in range(frames):
+                filter_frame(f, "near")
+                transform_part(f)
+
+    @pl.when(core == 0)
+    def _():
+        with jax.named_scope("far"):
+            split[0] = jnp.zeros(split.shape[1:], split.dtype)
+            for f in range(1, frames):
+                filter_frame(f, "far")
+                transform_part(f)
+
     with jax.named_scope("barrier"):
         pl.semaphore_wait(barrier, total - 1)
-    for g in range(TAPS - 1):
-        halo_copy(g).start()
+
+    @pl.when(core == 1)
+    def _():
+        for g in range(TAPS - 1):
+            halo_copy(g).start()
+        for f in range(frames):
+            part_copy(f).start()
+
+    @pl.when(core == 0)
+    def _():
+        for f in range(1, frames):
+            part_copy(f).start()
+        levels = [lax.rem(z + u, n_z) for u in range(n_z)]
+        for f in range(frames):
+            if f:
+                with jax.named_scope(f"halo{f}"):
+                    halo_copy(f - 1).wait_recv()
+            with jax.named_scope(f"whole{f}"):
+                filter_frame(f, "full")
+                transform_whole(f)
+            if f % PAIR == PAIR - 1:
+                c = f // PAIR
+                with jax.named_scope(f"ship{f}"):
+                    ship(send, [c * total + v * owners for v in levels], levels, tm, c, s_sem)
 
     def steer(i, carry):
         at = pl.ds(pl.multiple_of(i * step_rows, step_rows), step_rows)
@@ -256,16 +335,24 @@
 
     with jax.named_scope("steer"):
         lax.fori_loop(0, inputs // step_rows, steer, 0)
-    for f in range(1, frames):
-        with jax.named_scope(f"halo{f}"):
-            halo_ready(f - 1)
-        with jax.named_scope(f"filter{f}"):
-            filter_frame(f)
-        with jax.named_scope(f"transform{f}"):
-            transform_frame(f)
+
+    for f in range(frames):
+        with jax.named_scope(f"part{f}"):
+            if f:
+                part_copy(f).wait_recv()
+            else:
+
+                @pl.when(core == 0)
+                def _():
+                    part_copy(0).wait_recv()
+
+        with jax.named_scope(f"combine{f}"):
+            combine(f)
         if f % PAIR == PAIR - 1:
-            with jax.named_scope(f"ship{f}"):
-                ship(f // PAIR)
+            c = f // PAIR
+            with jax.named_scope(f"shipb{f}"):
+                starts = [(c * sides + t) * owners for t in range(sides)]
+                ship(send_b, starts, kept, source_tm, c, b_sem)
 
     for c in range(chunks - 1):
         with jax.named_scope("arrive"):
@@ -287,11 +374,25 @@
             lax.fori_loop(0, inputs // width, products, 0)
     with jax.named_scope("final"):
         arrived(chunks - 1)
+
     with jax.named_scope("left"):
         for c in range(chunks):
-            left(c)
-        for g in range(TAPS - 1):
-            halo_copy(g).wait_send()
+            some = pl.ds(0, sides * owners - 1)
+            pltpu.make_async_copy(send_b.at[some], send_b.at[some], b_sem.at[c]).wait()
+        for f in range(1, frames):
+            part_copy(f).wait_send()
+
+        @pl.when(core == 1)
+        def _():
+            part_copy(0).wait_send()
+            for g in range(TAPS - 1):
+                halo_copy(g).wait_send()
+
+        @pl.when(core == 0)
+        def _():
+            for c in range(chunks):
+                some = pl.ds(0, total - 1)
+                pltpu.make_async_copy(send.at[some], send.at[some], s_sem.at[c]).wait()
 
 
 def exchange(volt, gain, feed, grid, n_time, n_inp):
@@ -326,7 +427,11 @@
             pltpu.VMEM((rows, L), jnp.bfloat16),
             pltpu.VMEM((rows // LANES, 2 * CH * PAIR, LANES), jnp.float32),
             pltpu.VMEM((blocks, 8, rows), jnp.bfloat16),
+            pltpu.VMEM((blocks // 2, 8, rows), jnp.bfloat16),
             pltpu.VMEM((rows, (TAPS - 1) * L), jnp.bfloat16),
+            pltpu.VMEM((frames, 2 * CH, rows), jnp.float32),
+            pltpu.VMEM((frames, n_inp, CH // n_inp, rows), jnp.bfloat16),
+            pltpu.VMEM((frames, n_inp, CH // n_inp, rows), jnp.bfloat16),
             pltpu.VMEM((rows, LANES), jnp.float32),
             pltpu.VMEM((inputs, LANES), jnp.int32),
             pltpu.VMEM((2, depth, inputs), jnp.bfloat16),
@@ -335,13 +440,15 @@
             pltpu.VMEM((2, inputs, depth), jnp.bfloat16),
             dma((chunks,)),
             dma((chunks,)),
+            dma((chunks,)),
             dma((TAPS - 1,)),
             dma((TAPS - 1,)),
-            dma((chunks,)),
+            dma((frames,)),
+            dma((frames,)),
             dma((6,)),
         ],
-        compiler_params=pltpu.CompilerParams(collective_id=0, has_side_effects=True, vmem_limit_bytes=24 << 20),
-    )(*(pltpu.with_memory_space_constraint(a, pltpu.HBM) for a in (volt, gain, jnp.asarray(window_table()), jnp.asarray(dft_table()), feed, grid)))
+        compiler_params=pltpu.CompilerParams(collective_id=0, has_side_effects=True, vmem_limit_bytes=30 << 20),
+    )(*(pltpu.with_memory_space_constraint(a, pltpu.HBM) for a in (volt, gain, jnp.asarray(window_table()), jnp.asarray(dft_table(n_time, n_inp)), feed, grid)))
 
 
 def products_kernel(n_time, n_inp, recv, cosine, sine, sums, part, visible, power, spec, turn, spec_t, turn_t):

time: 89.2 us -> 80.5 us (0.902)
  Pallas kernels: 88.4 us -> 79.8 us
    pallas_call x1, Pallas kernels: 79.9 us -> 71.2 us  [exchange(): pl.pallas_call(functools.partial(exchange_kernel, n_time, n_inp), name='e...]
where the time goes in v3:
time: 80.5 us; the launch traced here: 80.4 us
  Pallas kernels  79.8 us (99%)
    pallas_call x1, Pallas kernels, exchange(): pl.pallas_call(functools.partial(exchange_kernel, n_time, n_inp), name='e...  71.2 us
    pallas_call x1, Pallas kernels, products(): pl.pallas_call(functools.partial(products_kernel, n_time, n_inp), name='p...  8.61 us

profile of v3, /device:TPU:1, one launch (start us, length us, event | category | flops | bytes accessed | tf_op | source)
XLA Modules:
  0.0 80.4 jit_solution(761295708378887227)
XLA Ops:
  0.6 71.2 %exchange.1 = (bf16[512,8,256]{2,1,0:T(8,128)(2,1)S(1)}, bf16[1024,1024]{1,0:T(8,128)(2,1)S(1)}, bf16[1024,1024]{1,0:T(8,128)(2,1)S(1)}, f32[2,2,1024,1024]{3,2,1,0:T(8,128)S(1)}, f32[2,1,1024]{2,1,0:T(1,128)S(1)}) custom-call(bf16[256,4096]{1,0:T(8,128)(2,1)} %volt_h.1, f32[1,256]{1,0:T(1,128)} %bitcast.5, f32[4,1024]{1,0:T(4,128)} %constant.4.clone.window_h, ...), custom_call_target="tpu_custom_call" | custom-call | tf_op jit(solution)/shard_map/exchange/pallas_call | solution.py:408
  71.8 8.6 %products.1 = (bf16[2,2,1024,1024]{3,2,1,0:T(8,128)(2,1)}, f32[2,1024]{1,0:T(2,128)}) custom-call(bf16[512,8,256]{2,1,0:T(8,128)(2,1)S(1)} %get-tuple-element.7.recv, bf16[1024,1024]{1,0:T(8,128)(2,1)S(1)} %get-tuple-element.8.cosine, bf16[1024,1024]{1,0:T(8,128)(2,1)S(1)} %get-tuple-element.9.sine, f32[2,2,1024,1024]{3,2,1,0:T(8,128)S(1)} %get-tuple-element.10.sums, ...), custom_call_target="tpu_custom_call" | custom-call | tf_op jit(solution)/shard_map/products/pallas_call | solution.py:477

commit v4 on v3

--- a/solution.py
+++ b/solution.py
@@ -301,6 +301,11 @@
     with jax.named_scope("barrier"):
         pl.semaphore_wait(barrier, total - 1)
 
+    def ship_whole(c):
+        levels = [lax.rem(z + u, n_z) for u in range(n_z)]
+        with jax.named_scope(f"ship{c}"):
+            ship(send, [c * total + v * owners for v in levels], levels, tm, c, s_sem)
+
     @pl.when(core == 1)
     def _():
         for g in range(TAPS - 1):
@@ -312,7 +317,6 @@
     def _():
         for f in range(1, frames):
             part_copy(f).start()
-        levels = [lax.rem(z + u, n_z) for u in range(n_z)]
         for f in range(frames):
             if f:
                 with jax.named_scope(f"halo{f}"):
@@ -320,10 +324,8 @@
             with jax.named_scope(f"whole{f}"):
                 filter_frame(f, "full")
                 transform_whole(f)
-            if f % PAIR == PAIR - 1:
-                c = f // PAIR
-                with jax.named_scope(f"ship{f}"):
-                    ship(send, [c * total + v * owners for v in levels], levels, tm, c, s_sem)
+            if f == PAIR - 1:
+                ship_whole(0)
 
     def steer(i, carry):
         at = pl.ds(pl.multiple_of(i * step_rows, step_rows), step_rows)
@@ -333,9 +335,6 @@
         sine[at, :] = s
         return carry
 
-    with jax.named_scope("steer"):
-        lax.fori_loop(0, inputs // step_rows, steer, 0)
-
     for f in range(frames):
         with jax.named_scope(f"part{f}"):
             if f:
@@ -353,6 +352,15 @@
             with jax.named_scope(f"shipb{f}"):
                 starts = [(c * sides + t) * owners for t in range(sides)]
                 ship(send_b, starts, kept, source_tm, c, b_sem)
+            if c + 1 < chunks:
+
+                @pl.when(core == 0)
+                def _():
+                    ship_whole(c + 1)
+
+            if c == 0:
+                with jax.named_scope("steer"):
+                    lax.fori_loop(0, inputs // step_rows, steer, 0)
 
     for c in range(chunks - 1):
         with jax.named_scope("arrive"):

time: 80.5 us -> 81.6 us (1.014); the launches traced: 80.4 us -> 80.3 us
  no operation moved by 1% of the time
where the time goes in v4:
time: 81.6 us; the launch traced here: 80.3 us
  Pallas kernels  79.7 us (98%)
    pallas_call x1, Pallas kernels, exchange(): pl.pallas_call(functools.partial(exchange_kernel, n_time, n_inp), name='e...  71.1 us
    pallas_call x1, Pallas kernels, products(): pl.pallas_call(functools.partial(products_kernel, n_time, n_inp), name='p...  8.62 us

profile of v4, /device:TPU:1, one launch (start us, length us, event | category | flops | bytes accessed | tf_op | source)
XLA Modules:
  0.0 80.3 jit_solution(784479533712836782)
XLA Ops:
  0.6 71.1 %exchange.1 = (bf16[512,8,256]{2,1,0:T(8,128)(2,1)S(1)}, bf16[1024,1024]{1,0:T(8,128)(2,1)S(1)}, bf16[1024,1024]{1,0:T(8,128)(2,1)S(1)}, f32[2,2,1024,1024]{3,2,1,0:T(8,128)S(1)}, f32[2,1,1024]{2,1,0:T(1,128)S(1)}) custom-call(bf16[256,4096]{1,0:T(8,128)(2,1)} %volt_h.1, f32[1,256]{1,0:T(1,128)} %bitcast.5, f32[4,1024]{1,0:T(4,128)} %constant.4.clone.window_h, ...), custom_call_target="tpu_custom_call" | custom-call | tf_op jit(solution)/shard_map/exchange/pallas_call | solution.py:416
  71.7 8.6 %products.1 = (bf16[2,2,1024,1024]{3,2,1,0:T(8,128)(2,1)}, f32[2,1024]{1,0:T(2,128)}) custom-call(bf16[512,8,256]{2,1,0:T(8,128)(2,1)S(1)} %get-tuple-element.7.recv, bf16[1024,1024]{1,0:T(8,128)(2,1)S(1)} %get-tuple-element.8.cosine, bf16[1024,1024]{1,0:T(8,128)(2,1)S(1)} %get-tuple-element.9.sine, f32[2,2,1024,1024]{3,2,1,0:T(8,128)S(1)} %get-tuple-element.10.sums, ...), custom_call_target="tpu_custom_call" | custom-call | tf_op jit(solution)/shard_map/products/pallas_call | solution.py:485

commit v5 on v3

--- a/solution.py
+++ b/solution.py
@@ -161,9 +161,18 @@
         pl.semaphore_signal(barrier, inc=1, device_id=d, device_id_type=LOGICAL)
         return carry
 
+    plane = 4 * n_inp
+
+    def greet_plane(row, carry):
+        for i in range(plane):
+            greet(row * plane + i, carry)
+        return carry
+
     with jax.named_scope("greet"):
-        lax.fori_loop(me + 1, total, greet, 0)
-        lax.fori_loop(0, me, greet, 0)
+        lax.fori_loop(yx + 1, n_yx, greet_plane, 0)
+        lax.fori_loop(0, yx, greet_plane, 0)
+        lax.fori_loop(me + 1, (yx + 1) * plane, greet, 0)
+        lax.fori_loop(yx * plane, me, greet, 0)
 
     step_rows = 16
 
@@ -282,13 +291,25 @@
         gain_b[...] = jnp.broadcast_to(gain[...], (LANES, rows)).T
         feed_b[...] = jnp.broadcast_to(feed[...], (LANES, inputs)).T
 
+    def meet():
+        with jax.named_scope("barrier"):
+            pl.semaphore_wait(barrier, total - 1)
+
     @pl.when(core == 1)
     def _():
-        with jax.named_scope("near"):
-            inward[0] = jnp.zeros(inward.shape[1:], inward.dtype)
-            for f in range(frames):
+        inward[0] = jnp.zeros(inward.shape[1:], inward.dtype)
+        for f in range(frames):
+            with jax.named_scope(f"near{f}"):
                 filter_frame(f, "near")
                 transform_part(f)
+            if f == PAIR - 1:
+                meet()
+                for g in range(TAPS - 1):
+                    halo_copy(g).start()
+                for done in range(PAIR):
+                    part_copy(done).start()
+            elif f >= PAIR:
+                part_copy(f).start()
 
     @pl.when(core == 0)
     def _():
@@ -297,19 +318,7 @@
             for f in range(1, frames):
                 filter_frame(f, "far")
                 transform_part(f)
-
-    with jax.named_scope("barrier"):
-        pl.semaphore_wait(barrier, total - 1)
-
-    @pl.when(core == 1)
-    def _():
-        for g in range(TAPS - 1):
-            halo_copy(g).start()
-        for f in range(frames):
-            part_copy(f).start()
-
-    @pl.when(core == 0)
-    def _():
+        meet()
         for f in range(1, frames):
             part_copy(f).start()
         levels = [lax.rem(z + u, n_z) for u in range(n_z)]
@@ -471,7 +480,7 @@
 
 def products(recv, cosine, sine, sums, part, n_time, n_inp):
     inputs, beams = cosine.shape
-    width = 256
+    width = 512
     depth = n_time * 4
     vmem = pl.BlockSpec(memory_space=pltpu.VMEM)
     return pl.pallas_call(

time: 80.5 us -> 78.7 us (0.978)
  Pallas kernels: 79.8 us -> 78 us
    pallas_call x1, Pallas kernels: 8.61 us -> 7.25 us  [products(): pl.pallas_call(functools.partial(products_kernel, n_time, n_inp), name='p...]
where the time goes in v5:
time: 78.7 us; the launch traced here: 78.6 us
  Pallas kernels  78 us (99%)
    pallas_call x1, Pallas kernels, exchange(): pl.pallas_call(functools.partial(exchange_kernel, n_time, n_inp), name='e...  70.7 us
    pallas_call x1, Pallas kernels, products(): pl.pallas_call(functools.partial(products_kernel, n_time, n_inp), name='p...  7.25 us

profile of v5, /device:TPU:1, one launch (start us, length us, event | category | flops | bytes accessed | tf_op | source)
XLA Modules:
  0.0 78.6 jit_solution(13444456708411319544)
XLA Ops:
  0.6 70.7 %exchange.1 = (bf16[512,8,256]{2,1,0:T(8,128)(2,1)S(1)}, bf16[1024,1024]{1,0:T(8,128)(2,1)S(1)}, bf16[1024,1024]{1,0:T(8,128)(2,1)S(1)}, f32[2,2,1024,1024]{3,2,1,0:T(8,128)S(1)}, f32[2,1,1024]{2,1,0:T(1,128)S(1)}) custom-call(bf16[256,4096]{1,0:T(8,128)(2,1)} %volt_h.1, f32[1,256]{1,0:T(1,128)} %bitcast.5, f32[4,1024]{1,0:T(4,128)} %constant.4.clone.window_h, ...), custom_call_target="tpu_custom_call" | custom-call | tf_op jit(solution)/shard_map/exchange/pallas_call | solution.py:417
  71.4 7.2 %products.1 = (bf16[2,2,1024,1024]{3,2,1,0:T(8,128)(2,1)}, f32[2,1024]{1,0:T(2,128)}) custom-call(bf16[512,8,256]{2,1,0:T(8,128)(2,1)S(1)} %get-tuple-element.7.recv, bf16[1024,1024]{1,0:T(8,128)(2,1)S(1)} %get-tuple-element.8.cosine, bf16[1024,1024]{1,0:T(8,128)(2,1)S(1)} %get-tuple-element.9.sine, f32[2,2,1024,1024]{3,2,1,0:T(8,128)S(1)} %get-tuple-element.10.sums, ...), custom_call_target="tpu_custom_call" | custom-call | tf_op jit(solution)/shard_map/products/pallas_call | solution.py:486

commit v6 on v5

--- a/solution.py
+++ b/solution.py
@@ -286,10 +286,9 @@
         )
 
     with jax.named_scope("load"):
-        for load in loads:
+        for load in loads[:3]:
             load.wait()
         gain_b[...] = jnp.broadcast_to(gain[...], (LANES, rows)).T
-        feed_b[...] = jnp.broadcast_to(feed[...], (LANES, inputs)).T
 
     def meet():
         with jax.named_scope("barrier"):
@@ -301,6 +300,8 @@
         for f in range(frames):
             with jax.named_scope(f"near{f}"):
                 filter_frame(f, "near")
+                if f == 0:
+                    loads[5].wait()
                 transform_part(f)
             if f == PAIR - 1:
                 meet()
@@ -317,6 +318,8 @@
             split[0] = jnp.zeros(split.shape[1:], split.dtype)
             for f in range(1, frames):
                 filter_frame(f, "far")
+                if f == 1:
+                    loads[5].wait()
                 transform_part(f)
         meet()
         for f in range(1, frames):
@@ -343,6 +346,9 @@
         return carry
 
     with jax.named_scope("steer"):
+        for load in loads[3:5]:
+            load.wait()
+        feed_b[...] = jnp.broadcast_to(feed[...], (LANES, inputs)).T
         lax.fori_loop(0, inputs // step_rows, steer, 0)
 
     for f in range(frames):

time: 78.7 us -> 78.7 us (level)
  no operation moved by 1% of the time
where the time goes in v6:
time: 78.7 us; the launch traced here: 78.6 us
  Pallas kernels  78 us (99%)
    pallas_call x1, Pallas kernels, exchange(): pl.pallas_call(functools.partial(exchange_kernel, n_time, n_inp), name='e...  70.7 us
    pallas_call x1, Pallas kernels, products(): pl.pallas_call(functools.partial(products_kernel, n_time, n_inp), name='p...  7.25 us

profile of v6, /device:TPU:1, one launch (start us, length us, event | category | flops | bytes accessed | tf_op | source)
XLA Modules:
  0.0 78.6 jit_solution(12931146880314713198)
XLA Ops:
  0.6 70.7 %exchange.1 = (bf16[512,8,256]{2,1,0:T(8,128)(2,1)S(1)}, bf16[1024,1024]{1,0:T(8,128)(2,1)S(1)}, bf16[1024,1024]{1,0:T(8,128)(2,1)S(1)}, f32[2,2,1024,1024]{3,2,1,0:T(8,128)S(1)}, f32[2,1,1024]{2,1,0:T(1,128)S(1)}) custom-call(bf16[256,4096]{1,0:T(8,128)(2,1)} %volt_h.1, f32[1,256]{1,0:T(1,128)} %bitcast.5, f32[4,1024]{1,0:T(4,128)} %constant.4.clone.window_h, ...), custom_call_target="tpu_custom_call" | custom-call | tf_op jit(solution)/shard_map/exchange/pallas_call | solution.py:423
  71.4 7.2 %products.1 = (bf16[2,2,1024,1024]{3,2,1,0:T(8,128)(2,1)}, f32[2,1024]{1,0:T(2,128)}) custom-call(bf16[512,8,256]{2,1,0:T(8,128)(2,1)S(1)} %get-tuple-element.7.recv, bf16[1024,1024]{1,0:T(8,128)(2,1)S(1)} %get-tuple-element.8.cosine, bf16[1024,1024]{1,0:T(8,128)(2,1)S(1)} %get-tuple-element.9.sine, f32[2,2,1024,1024]{3,2,1,0:T(8,128)S(1)} %get-tuple-element.10.sums, ...), custom_call_target="tpu_custom_call" | custom-call | tf_op jit(solution)/shard_map/products/pallas_call | solution.py:492
